TPU v7x, 32 devices: a whole 2x2x4 slice. The times are simulated.
32 devices in a mesh: feat: 2 (over x), lat: 16 (over z, y, core).
Axes of the slice: x: 2, y: 2, z: 4, core: 2. Of those that a mesh axis runs over, the one named last changes fastest.
Arguments:
- acts: bfloat16 [2, 128, 4096], P(None, 'lat', 'feat'), may hold values from -6 to 6
- weight: bfloat16 [2, 4096, 16384], P(None, 'feat', 'lat'), may hold values from -0.0625 to 0.0625
- enc_bias: float32 [16384], P('lat'), may hold values from -1 to 0.5
- dec_bias: float32 [2, 4096], P(None, 'feat'), may hold values from -1 to 1
Outputs:
- grad_weight: bfloat16 [2, 4096, 16384], P(None, 'feat', 'lat')
- grad_enc_bias: float32 [16384], P('lat')
- grad_dec_bias: float32 [2, 4096], P(None, 'feat')
All inputs are finite; a program needn't handle non-finite values.
Results may differ from a plain program's by a relative error of at most 0.0085.
Values may be sent and summed in bfloat16 or wider, within the bound.
No kernel may reach another device: no remote copies, remote signals or barrier semaphores. Data moves between devices by JAX's collectives and lax.ppermute only.
A program may use at most 128 MiB of HBM per device.

v0:
```python
import math
import jax
import jax.numpy as jnp
from jax import lax
from jax.sharding import PartitionSpec as P


def channel_terms(left, right):
    first = jnp.dot(left[0], right[0], preferred_element_type=jnp.float32)
    return first + jnp.dot(left[1], right[1], preferred_element_type=jnp.float32)


def on_device(acts, weight, enc_bias, dec_bias):
    width = weight.shape[1] * lax.axis_size("feat")
    lats = weight.shape[2] * lax.axis_size("lat")
    scale = math.sqrt(2.0 * width / lats)
    whole_rows = lax.all_gather(acts, "lat", axis=1, tiled=True)
    partial_value = channel_terms(whole_rows, weight)
    pre_share = (
        lax.psum_scatter(
            partial_value.astype(jnp.bfloat16), "feat", scatter_dimension=0, tiled=True
        ).astype(jnp.float32)
        + enc_bias
    )
    act_share = jax.nn.softplus(pre_share).astype(jnp.bfloat16)
    latents = lax.all_gather(act_share, "feat", axis=0, tiled=True)
    recon_terms = jnp.einsum("rl,mdl->mrd", latents, weight, preferred_element_type=jnp.float32)
    summed = lax.psum(recon_terms, "lat")
    resid = scale * summed + dec_bias[:, None, :] - whole_rows.astype(jnp.float32)
    grad_dec_bias = jnp.sum(resid, axis=1)
    resid_rows = resid.astype(jnp.bfloat16)
    backed = channel_terms(resid_rows, weight)
    back_part = lax.psum_scatter(
        backed.astype(jnp.bfloat16), "feat", scatter_dimension=0, tiled=True
    ).astype(jnp.float32)
    grad_share = scale * back_part * jax.nn.sigmoid(pre_share)
    grad_enc_bias = lax.psum(jnp.sum(grad_share, axis=0), "feat")
    grad_pre_b = lax.all_gather(grad_share.astype(jnp.bfloat16), "feat", axis=0, tiled=True)
    enc_term = jnp.einsum("mrd,rl->mdl", whole_rows, grad_pre_b, preferred_element_type=jnp.float32)
    dec_term = jnp.einsum("mrd,rl->mdl", resid_rows, latents, preferred_element_type=jnp.float32)
    grad_weight = (enc_term + scale * dec_term).astype(jnp.bfloat16)
    return (grad_weight, grad_enc_bias, grad_dec_bias)


def solution(mesh):
    placed = (P(None, "lat", "feat"), P(None, "feat", "lat"), P("lat"), P(None, "feat"))
    return jax.shard_map(
        on_device,
        mesh=mesh,
        in_specs=placed,
        out_specs=(P(None, "feat", "lat"), P("lat"), P(None, "feat")),
        check_vma=False,
    )
```

profile of v0, /device:TPU:0, one launch (start us, length us, event | category | flops | bytes accessed | tf_op | source)
XLA Modules:
  0.0 249.5 jit_solution(9672463318507042027)
XLA Ops:
  7.2 0.0 copy-start.3
  7.2 0.0 all-gather.2.cloned.1.call-start
  7.2 0.7 all-gather.2.cloned.1.call-update
  7.9 0.0 reduce-scatter.3.cloned.1.call-start
  8.0 42.8 %all-gather.2.cloned.1.call-done = bf16[2,128,2048]{2,1,0:T(8,128)(2,1)} async-done(((bf16[2,8,2048]{2,1,0:T(8,128)(2,1)}), bf16[2,128,2048]{2,1,0:T(8,128)(2,1)}) %all-gather.2.cloned.1.call-update) | async-done | bytes 1048592 | tf_op jit(solution)/shard_map/all_gather | solution.py:17
  50.8 3.1 %fusion.3 = f32[128,1024]{1,0:T(8,128)S(1)} fusion(bf16[2,2048,1024]{2,1,0:T(8,128)(2,1)} %param.5, bf16[2,128,2048]{2,1,0:T(8,128)(2,1)} %all-gather.2.cloned.1.call-done), kind=kOutput, calls=%fused_computation.4 | convolution fusion | flops 536870912 | bytes 5242880 | tf_op jit(solution)/shard_map/dot_general | solution.py:10
  53.9 3.8 %fusion.22 = bf16[128,1024]{1,0:T(8,128)(2,1)} fusion(f32[128,1024]{1,0:T(8,128)S(1)} %fusion.3, bf16[2,2048,1024]{2,1,0:T(8,128)(2,1)} %param.5, bf16[2,128,2048]{2,1,0:T(8,128)(2,1)} %all-gather.2.cloned.1.call-done), kind=kOutput, calls=%fused_computation.19 | convolution fusion | flops 537133056 | bytes 5505024 | tf_op jit(solution)/shard_map/dot_general | solution.py:9
  57.6 0.0 copy-start
  57.7 0.0 copy-start.2
  57.7 0.0 reduce-scatter.3.cloned.1.call-update
  57.7 0.0 all-reduce.2.cloned.1.call-start
  57.7 10.8 %reduce-scatter.3.cloned.1.call-done = bf16[64,1024]{1,0:T(8,128)(2,1)} async-done(((bf16[128,1024]{1,0:T(8,128)(2,1)}), bf16[64,1024]{1,0:T(8,128)(2,1)}) %reduce-scatter.3.cloned.1.call-update) | async-done | bytes 131088 | tf_op jit(solution)/shard_map/reduce_scatter | solution.py:20
  68.6 0.0 copy-done.3
  68.6 1.1 fusion.27
  69.6 5.7 %all_gather.10 = bf16[128,1024]{1,0:T(8,128)(2,1)S(1)} all-gather(bf16[64,1024]{1,0:T(8,128)(2,1)S(1)} %fusion.27), channel_id=1, replica_groups=mesh['feat'=2,'lat'=16] {'feat'}, dimensions={0}, use_global_device_ids=true | all-gather | bytes 393216 | tf_op jit(solution)/shard_map/all_gather | solution.py:26
  75.4 7.6 %convolution_bitcast_fusion = f32[2,128,2048]{2,1,0:T(8,128)} fusion(bf16[2,2048,1024]{2,1,0:T(8,128)(2,1)} %param.5, bf16[128,1024]{1,0:T(8,128)(2,1)S(1)} %all_gather.10), kind=kOutput, calls=%fused_computation.14 | convolution fusion | flops 1073741824 | bytes 10747904 | tf_op jit(solution)/shard_map/rl,mdl->mrd/dot_general | solution.py:27
  82.9 0.0 all-reduce.2.cloned.1.call-update
  82.9 0.0 copy-start.1
  83.0 0.0 reduce-scatter.5.cloned.1.call-start
  83.0 98.1 %all-reduce.2.cloned.1.call-done = f32[2,128,2048]{2,1,0:T(8,128)} async-done(((f32[2,128,2048]{2,1,0:T(8,128)}), f32[2,128,2048]{2,1,0:T(8,128)}) %all-reduce.2.cloned.1.call-update) | async-done | bytes 2097168 | tf_op jit(solution)/shard_map/psum | solution.py:28
  181.1 0.0 copy-done
  181.1 0.0 copy-done.2
  181.1 2.6 %fusion.25 = (f32[2,2048]{1,0:T(2,128)}, bf16[2,128,2048]{2,1,0:T(8,128)(2,1)S(1)}) fusion(bf16[2,128,2048]{2,1,0:T(8,128)(2,1)S(1)} %copy-done, f32[2,128,2048]{2,1,0:T(8,128)} %all-reduce.2.cloned.1.call-done, f32[2,2048]{1,0:T(2,128)S(1)} %copy-done.2), kind=kLoop, calls=%fused_computation.20 | loop fusion | flops 3141632 | bytes 4227072 | tf_op jit(solution)/shard_map/reduce_sum | solution.py:30
  183.8 2.9 %fusion.1 = f32[128,1024]{1,0:T(8,128)S(1)} fusion(bf16[2,2048,1024]{2,1,0:T(8,128)(2,1)} %param.5, bf16[2,128,2048]{2,1,0:T(8,128)(2,1)S(1)} %get-tuple-element.7), kind=kOutput, calls=%fused_computation.2 | convolution fusion | flops 536870912 | bytes 5242880 | tf_op jit(solution)/shard_map/dot_general | solution.py:10
  186.7 3.6 %fusion.19 = bf16[128,1024]{1,0:T(8,128)(2,1)} fusion(f32[128,1024]{1,0:T(8,128)S(1)} %fusion.1, bf16[2,2048,1024]{2,1,0:T(8,128)(2,1)} %param.5, bf16[2,128,2048]{2,1,0:T(8,128)(2,1)S(1)} %get-tuple-element.7), kind=kOutput, calls=%fused_computation.18 | convolution fusion | flops 537133056 | bytes 5505024 | tf_op jit(solution)/shard_map/dot_general | solution.py:9
  190.3 0.0 reduce-scatter.5.cloned.1.call-update
  190.3 11.4 %reduce-scatter.5.cloned.1.call-done = bf16[64,1024]{1,0:T(8,128)(2,1)} async-done(((bf16[128,1024]{1,0:T(8,128)(2,1)}), bf16[64,1024]{1,0:T(8,128)(2,1)}) %reduce-scatter.5.cloned.1.call-update) | async-done | bytes 131088 | tf_op jit(solution)/shard_map/reduce_scatter | solution.py:33
  201.7 0.0 copy-done.1
  201.7 1.0 fusion.32
  202.7 5.5 %psum.15 = f32[1024]{0:T(1024)} all-reduce(f32[1024]{0:T(1024)S(1)} %get-tuple-element.8), channel_id=1, replica_groups=mesh['feat'=2,'lat'=16] {'feat'}, use_global_device_ids=true, to_apply=%region_4.5 | all-reduce | flops 1024 | bytes 8192 | tf_op jit(solution)/shard_map/psum | solution.py:37
  208.2 5.6 %all_gather.11 = bf16[128,1024]{1,0:T(8,128)(2,1)S(1)} all-gather(bf16[64,1024]{1,0:T(8,128)(2,1)S(1)} %get-tuple-element.9), channel_id=1, replica_groups=mesh['feat'=2,'lat'=16] {'feat'}, dimensions={0}, use_global_device_ids=true | all-gather | bytes 393216 | tf_op jit(solution)/shard_map/all_gather | solution.py:38
  213.9 8.1 %fusion.28 = f32[1024,2,2048]{2,0,1:T(8,128)} fusion(bf16[2,128,2048]{2,1,0:T(8,128)(2,1)S(1)} %copy-done, bf16[128,1024]{1,0:T(8,128)(2,1)S(1)} %all_gather.11), kind=kOutput, calls=%fused_computation.28 | convolution fusion | flops 1073741824 | bytes 18087936 | tf_op jit(solution)/shard_map/mrd,rl->mdl/dot_general | solution.py:39
  222.0 9.2 %fusion = bf16[2,2048,1024]{1,2,0:T(8,128)(2,1)} fusion(f32[1024,2,2048]{2,0,1:T(8,128)} %fusion.28, bf16[2,128,2048]{2,1,0:T(8,128)(2,1)S(1)} %get-tuple-element.7, bf16[128,1024]{1,0:T(8,128)(2,1)S(1)} %all_gather.10), kind=kOutput, calls=%fused_computation.1 | convolution fusion | flops 1086324736 | bytes 26476544 | tf_op jit(solution)/shard_map/mrd,rl->mdl/dot_general | solution.py:40
  231.2 11.8 %copy.9 = bf16[2,2048,1024]{2,1,0:T(8,128)(2,1)} copy(bf16[2,2048,1024]{1,2,0:T(8,128)(2,1)} %fusion) | data formatting | bytes 16777216
Async XLA Ops:
  7.2 61.4 %copy-start.3 = (f32[1024]{0:T(1024)S(1)}, f32[1024]{0:T(1024)}, u32[]{:S(2)}) copy-start(f32[1024]{0:T(1024)} %param.6) | copy-start | bytes 12292
  7.2 43.6 %all-gather.2.cloned.1.call-start = ((), (), s32[]{:S(2)}) async-start(), calls=%async_computation.2 | async-start | bytes 1114112 | tf_op jit(solution)/shard_map/all_gather | solution.py:17
  7.9 60.7 %reduce-scatter.3.cloned.1.call-start = ((), (), s32[]{:S(2)}) async-start(), calls=%async_computation.3 | async-start | bytes 393216 | tf_op jit(solution)/shard_map/reduce_scatter | solution.py:20
  57.6 123.5 %copy-start = (bf16[2,128,2048]{2,1,0:T(8,128)(2,1)S(1)}, bf16[2,128,2048]{2,1,0:T(8,128)(2,1)}, u32[]{:S(2)}) copy-start(bf16[2,128,2048]{2,1,0:T(8,128)(2,1)} %all-gather.2.cloned.1.call-done) | copy-start | bytes 3145732
  57.7 123.5 %copy-start.2 = (f32[2,2048]{1,0:T(2,128)S(1)}, f32[2,2048]{1,0:T(2,128)}, u32[]{:S(2)}) copy-start(f32[2,2048]{1,0:T(2,128)} %param.7) | copy-start | bytes 49156
  57.7 123.5 %all-reduce.2.cloned.1.call-start = ((), (), s32[]{:S(2)}) async-start(), calls=%async_computation.4 | async-start | bytes 4194304 | tf_op jit(solution)/shard_map/psum | solution.py:28
  82.9 118.8 %copy-start.1 = (bf16[64,1024]{1,0:T(8,128)(2,1)S(1)}, bf16[64,1024]{1,0:T(8,128)(2,1)}, u32[]{:S(2)}) copy-start(bf16[64,1024]{1,0:T(8,128)(2,1)} %reduce-scatter.3.cloned.1.call-done) | copy-start | bytes 393220
  83.0 118.8 %reduce-scatter.5.cloned.1.call-start = ((), (), s32[]{:S(2)}) async-start(), calls=%async_computation.5 | async-start | bytes 393216 | tf_op jit(solution)/shard_map/reduce_scatter | solution.py:33
Sparse Core Ops, SparseCore 0:
  10.2 40.5 all-gather.1
  57.8 10.7 reduce-scatter.2
  83.1 98.0 all-reduce.1
  190.5 11.2 reduce-scatter.4
where the time goes:
time: 250 us
  waiting for transfers between devices  164 us (66%)
  matrix products  38.2 us (15%)
  blocking collectives  16.9 us (7%)
  between operations  13.8 us (6%)
  local copies, waits for them, and re-layouts  11.8 us (5%)
  other arithmetic  4.72 us (2%)
    psum x1, waiting for transfers between devices, on_device(): summed = lax.psum(recon_terms, 'lat')  98.1 us
    all_gather x1, waiting for transfers between devices, on_device(): whole_rows = lax.all_gather(acts, 'lat', axis=1, tiled=True)  42.8 us
    unnamed x9, local copies, waits for them, and re-layouts  11.8 us
    reduce_scatter x1, waiting for transfers between devices, on_device(): lax.psum_scatter(backed.astype(jnp.bfloat16), 'feat', scatter_dimension=0...  11.4 us
    reduce_scatter x1, waiting for transfers between devices, on_device(): lax.psum_scatter(partial_value.astype(jnp.bfloat16), 'feat', scatter_dime...  10.8 us
    dot_general x1, matrix products, on_device(): jnp.einsum('mrd,rl->mdl', resid_rows, latents, preferred_element_type=jnp...  9.21 us
    dot_general x1, matrix products, on_device(): jnp.einsum('mrd,rl->mdl', whole_rows, grad_pre_b, preferred_element_type=...  8.09 us
    dot_general x1, matrix products, on_device(): jnp.einsum('rl,mdl->mrd', latents, weight, preferred_element_type=jnp.flo...  7.56 us
  transfers between devices with their start and end apart: 4, of which 4 were waited for; matrix products, arithmetic and copies ran while one was open for 0% of the time, Pallas kernels for 0%

commit v1 on v0

--- a/solution.py
+++ b/solution.py
@@ -3,6 +3,15 @@
 import jax.numpy as jnp
 from jax import lax
 from jax.sharding import PartitionSpec as P
+
+
+def add_in_pairs(block, mesh_axis):
+    n_dev = lax.axis_size(mesh_axis)
+    result, far = (block, 1)
+    while far < n_dev:
+        result = result + lax.ppermute(result, mesh_axis, [(i, i ^ far) for i in range(n_dev)])
+        far = 2 * far
+    return result
 
 
 def channel_terms(left, right):
@@ -25,7 +34,7 @@
     act_share = jax.nn.softplus(pre_share).astype(jnp.bfloat16)
     latents = lax.all_gather(act_share, "feat", axis=0, tiled=True)
     recon_terms = jnp.einsum("rl,mdl->mrd", latents, weight, preferred_element_type=jnp.float32)
-    summed = lax.psum(recon_terms, "lat")
+    summed = add_in_pairs(recon_terms, "lat")
     resid = scale * summed + dec_bias[:, None, :] - whole_rows.astype(jnp.float32)
     grad_dec_bias = jnp.sum(resid, axis=1)
     resid_rows = resid.astype(jnp.bfloat16)

time: 250 us -> 337 us (1.35)
  waiting for transfers between devices: 164 us -> 251 us
  matrix products: 38.2 us -> 32.5 us
  starting transfers between devices: 0.16 us -> 5.76 us
    ppermute x0 -> x4, waiting for transfers between devices: none -> 185 us  [add_in_pairs(): lax.ppermute(result, mesh_axis, [(i, i ^ far) for i in range(n_dev)])]
    psum x1 -> x0, waiting for transfers between devices: 98.1 us -> none  [on_device(): summed = lax.psum(recon_terms, 'lat')]
    ppermute x0 -> x4, starting transfers between devices: none -> 5.64 us  [add_in_pairs(): lax.ppermute(result, mesh_axis, [(i, i ^ far) for i in range(n_dev)])]
    unnamed x9 -> x13, local copies, waits for them, and re-layouts: 11.8 us -> 11.9 us
  transfers between devices with their start and end apart: 4 -> 7, of which waited for: 4 -> 7; matrix products, arithmetic and copies ran while one was open for 0% -> 0% of each run, Pallas kernels for 0% -> 0%
where the time goes in v1:
time: 337 us
  waiting for transfers between devices  251 us (74%)
  matrix products  32.5 us (10%)
  blocking collectives  16.9 us (5%)
  between operations  13.8 us (4%)
  local copies, waits for them, and re-layouts  11.9 us (4%)
  starting transfers between devices  5.76 us (2%)
  other arithmetic  4.33 us (1%)
    ppermute x4, waiting for transfers between devices, add_in_pairs(): lax.ppermute(result, mesh_axis, [(i, i ^ far) for i in range(n_dev)])  185 us
    all_gather x1, waiting for transfers between devices, on_device(): whole_rows = lax.all_gather(acts, 'lat', axis=1, tiled=True)  42.8 us
    reduce_scatter x1, waiting for transfers between devices, on_device(): lax.psum_scatter(backed.astype(jnp.bfloat16), 'feat', scatter_dimension=0...  11.9 us
    unnamed x13, local copies, waits for them, and re-layouts  11.9 us
    reduce_scatter x1, waiting for transfers between devices, on_device(): lax.psum_scatter(partial_value.astype(jnp.bfloat16), 'feat', scatter_dime...  10.8 us
    dot_general x1, matrix products, on_device(): jnp.einsum('mrd,rl->mdl', resid_rows, latents, preferred_element_type=jnp...  9.22 us
    dot_general x1, matrix products, on_device(): jnp.einsum('mrd,rl->mdl', whole_rows, grad_pre_b, preferred_element_type=...  8.11 us
  transfers between devices with their start and end apart: 7, of which 7 were waited for; matrix products, arithmetic and copies ran while one was open for 0% of the time, Pallas kernels for 0%

profile of v1, /device:TPU:0, one launch (start us, length us, event | category | flops | bytes accessed | tf_op | source)
XLA Modules:
  0.0 336.5 jit_solution(15866853445695223058)
XLA Ops:
  7.2 0.0 all-gather.2.cloned.1.call-start
  7.2 0.7 all-gather.2.cloned.1.call-update
  7.9 0.0 reduce-scatter.3.cloned.1.call-start
  7.9 42.8 %all-gather.2.cloned.1.call-done = bf16[2,128,2048]{2,1,0:T(8,128)(2,1)} async-done(((bf16[2,8,2048]{2,1,0:T(8,128)(2,1)}), bf16[2,128,2048]{2,1,0:T(8,128)(2,1)}) %all-gather.2.cloned.1.call-update) | async-done | bytes 1048592 | tf_op jit(solution)/shard_map/all_gather | solution.py:26
  50.8 0.0 copy-start
  50.8 3.1 fusion.3
  53.9 0.0 copy-done
  53.9 0.0 copy-start.3
  53.9 3.6 %fusion.22 = bf16[128,1024]{1,0:T(8,128)(2,1)} fusion(f32[128,1024]{1,0:T(8,128)S(1)} %fusion.3, bf16[2,2048,1024]{2,1,0:T(8,128)(2,1)} %param.5, bf16[2,128,2048]{2,1,0:T(8,128)(2,1)S(1)} %copy-done), kind=kOutput, calls=%fused_computation.19 | convolution fusion | flops 537133056 | bytes 5505024 | tf_op jit(solution)/shard_map/dot_general | solution.py:18
  57.6 0.0 reduce-scatter.3.cloned.1.call-update
  57.6 0.0 reduce-scatter.5.cloned.1.call-start
  57.6 10.8 %reduce-scatter.3.cloned.1.call-done = bf16[64,1024]{1,0:T(8,128)(2,1)} async-done(((bf16[128,1024]{1,0:T(8,128)(2,1)}), bf16[64,1024]{1,0:T(8,128)(2,1)}) %reduce-scatter.3.cloned.1.call-update) | async-done | bytes 131088 | tf_op jit(solution)/shard_map/reduce_scatter | solution.py:29
  68.5 0.0 copy-done.3
  68.5 1.1 fusion.25
  69.6 5.7 %all_gather.10 = bf16[128,1024]{1,0:T(8,128)(2,1)S(1)} all-gather(bf16[64,1024]{1,0:T(8,128)(2,1)S(1)} %fusion.25), channel_id=1, replica_groups=mesh['feat'=2,'lat'=16] {'feat'}, dimensions={0}, use_global_device_ids=true | all-gather | bytes 393216 | tf_op jit(solution)/shard_map/all_gather | solution.py:35
  75.3 6.2 %convolution_bitcast_fusion = f32[2,128,2048]{2,1,0:T(8,128)S(1)} fusion(bf16[2,2048,1024]{2,1,0:T(8,128)(2,1)} %param.5, bf16[128,1024]{1,0:T(8,128)(2,1)S(1)} %all_gather.10), kind=kOutput, calls=%fused_computation.14 | convolution fusion | flops 1073741824 | bytes 10747904 | tf_op jit(solution)/shard_map/rl,mdl->mrd/dot_general | solution.py:36
  81.5 0.1 collective-permute-start
  81.6 4.1 %collective-permute-done = f32[2,128,2048]{2,1,0:T(8,128)S(1)} collective-permute-done((f32[2,128,2048]{2,1,0:T(8,128)S(1)}, f32[2,128,2048]{2,1,0:T(8,128)S(1)}, u32[]{:S(2)}, u32[]{:S(2)}) %collective-permute-start) | collective-permute-done | bytes 2097184 | tf_op jit(solution)/shard_map/ppermute | solution.py:12
  85.7 0.3 add.54
  86.1 1.5 collective-permute-start.1
  87.6 46.2 %collective-permute-done.1 = f32[2,128,2048]{2,1,0:T(8,128)S(1)} collective-permute-done((f32[2,128,2048]{2,1,0:T(8,128)S(1)}, f32[2,128,2048]{2,1,0:T(8,128)S(1)}, u32[]{:S(2)}, u32[]{:S(2)}) %collective-permute-start.1) | collective-permute-done | bytes 2097184 | tf_op jit(solution)/shard_map/ppermute | solution.py:12
  133.8 0.0 slice-start
  133.8 0.3 add.55
  134.2 0.0 copy-start.2
  134.2 0.0 slice-start.1
  134.2 1.6 collective-permute-start.2
  135.8 45.3 %collective-permute-done.2 = f32[2,128,2048]{2,1,0:T(8,128)S(1)} collective-permute-done((f32[2,128,2048]{2,1,0:T(8,128)S(1)}, f32[2,128,2048]{2,1,0:T(8,128)S(1)}, u32[]{:S(2)}, u32[]{:S(2)}) %collective-permute-start.2) | collective-permute-done | bytes 2097184 | tf_op jit(solution)/shard_map/ppermute | solution.py:12
  181.1 0.3 add.56
  181.4 2.5 collective-permute-start.3
  183.9 89.4 %collective-permute-done.3 = f32[2,128,2048]{2,1,0:T(8,128)S(1)} collective-permute-done((f32[2,128,2048]{2,1,0:T(8,128)S(1)}, f32[2,128,2048]{2,1,0:T(8,128)S(1)}, u32[]{:S(2)}, u32[]{:S(2)}) %collective-permute-start.3) | collective-permute-done | bytes 2097184 | tf_op jit(solution)/shard_map/ppermute | solution.py:12
  273.3 0.0 copy-done.2
  273.3 1.2 fusion.30
  274.5 0.0 slice-done
  274.5 0.0 slice-done.1
  274.5 0.7 fusion.1
  275.3 0.0 copy-start.1
  275.3 1.5 fusion.19
  276.8 0.0 reduce-scatter.5.cloned.1.call-update
  276.8 11.9 %reduce-scatter.5.cloned.1.call-done = bf16[64,1024]{1,0:T(8,128)(2,1)} async-done(((bf16[128,1024]{1,0:T(8,128)(2,1)}), bf16[64,1024]{1,0:T(8,128)(2,1)}) %reduce-scatter.5.cloned.1.call-update) | async-done | bytes 131088 | tf_op jit(solution)/shard_map/reduce_scatter | solution.py:42
  288.7 0.0 copy-done.1
  288.7 1.0 fusion.32
  289.7 5.5 %psum.7 = f32[1024]{0:T(1024)} all-reduce(f32[1024]{0:T(1024)S(1)} %get-tuple-element.8), channel_id=1, replica_groups=mesh['feat'=2,'lat'=16] {'feat'}, use_global_device_ids=true, to_apply=%region_3.4 | all-reduce | flops 1024 | bytes 8192 | tf_op jit(solution)/shard_map/psum | solution.py:46
  295.2 5.6 %all_gather.11 = bf16[128,1024]{1,0:T(8,128)(2,1)S(1)} all-gather(bf16[64,1024]{1,0:T(8,128)(2,1)S(1)} %get-tuple-element.9), channel_id=1, replica_groups=mesh['feat'=2,'lat'=16] {'feat'}, dimensions={0}, use_global_device_ids=true | all-gather | bytes 393216 | tf_op jit(solution)/shard_map/all_gather | solution.py:47
  300.9 8.1 %fusion.26 = f32[1024,2,2048]{2,0,1:T(8,128)} fusion(bf16[2,128,2048]{2,1,0:T(8,128)(2,1)S(1)} %copy-done, bf16[128,1024]{1,0:T(8,128)(2,1)S(1)} %all_gather.11), kind=kOutput, calls=%fused_computation.26 | convolution fusion | flops 1073741824 | bytes 18087936 | tf_op jit(solution)/shard_map/mrd,rl->mdl/dot_general | solution.py:48
  309.0 9.2 %fusion = bf16[2,2048,1024]{1,2,0:T(8,128)(2,1)} fusion(f32[1024,2,2048]{2,0,1:T(8,128)} %fusion.26, bf16[2,128,2048]{2,1,0:T(8,128)(2,1)S(1)} %get-tuple-element.7, bf16[128,1024]{1,0:T(8,128)(2,1)S(1)} %all_gather.10), kind=kOutput, calls=%fused_computation.1 | convolution fusion | flops 1086324736 | bytes 26476544 | tf_op jit(solution)/shard_map/mrd,rl->mdl/dot_general | solution.py:49
  318.2 11.8 %copy.9 = bf16[2,2048,1024]{2,1,0:T(8,128)(2,1)} copy(bf16[2,2048,1024]{1,2,0:T(8,128)(2,1)} %fusion) | data formatting | bytes 16777216
  (1 shorter events, 0.0 us)
Async XLA Ops:
  7.2 43.6 %all-gather.2.cloned.1.call-start = ((), (), s32[]{:S(2)}) async-start(), calls=%async_computation.2 | async-start | bytes 1114112 | tf_op jit(solution)/shard_map/all_gather | solution.py:26
  7.9 60.6 %reduce-scatter.3.cloned.1.call-start = ((), (), s32[]{:S(2)}) async-start(), calls=%async_computation.3 | async-start | bytes 393216 | tf_op jit(solution)/shard_map/reduce_scatter | solution.py:29
  50.8 3.2 copy-start
  53.9 14.5 %copy-start.3 = (f32[1024]{0:T(1024)S(1)}, f32[1024]{0:T(1024)}, u32[]{:S(2)}) copy-start(f32[1024]{0:T(1024)} %param.6) | copy-start | bytes 12292
  57.6 231.1 %reduce-scatter.5.cloned.1.call-start = ((), (), s32[]{:S(2)}) async-start(), calls=%async_computation.4 | async-start | bytes 393216 | tf_op jit(solution)/shard_map/reduce_scatter | solution.py:42
  81.5 4.2 %collective-permute-start = (f32[2,128,2048]{2,1,0:T(8,128)S(1)}, f32[2,128,2048]{2,1,0:T(8,128)S(1)}, u32[]{:S(2)}, u32[]{:S(2)}) collective-permute-start(f32[2,128,2048]{2,1,0:T(8,128)S(1)} %convolution_bitcast_fusion), channel_id=1, source_target_pairs={{0,1},{1,0},{2,3},{3,2},{4,5},{5,4},{6,7},{7,6},{8,9},{9,8},{10,11... | collective-permute-start | bytes 6291464 | tf_op jit(solution)/shard_map/ppermute | solution.py:12
  86.1 47.7 %collective-permute-start.1 = (f32[2,128,2048]{2,1,0:T(8,128)S(1)}, f32[2,128,2048]{2,1,0:T(8,128)S(1)}, u32[]{:S(2)}, u32[]{:S(2)}) collective-permute-start(f32[2,128,2048]{2,1,0:T(8,128)S(1)} %add.54), channel_id=1, source_target_pairs={{0,2},{1,3},{2,0},{3,1},{4,6},{5,7},{6,4},{7,5},{8,10},{9,11},{10,... | collective-permute-start | bytes 6291464 | tf_op jit(solution)/shard_map/ppermute | solution.py:12
  133.8 140.7 %slice-start = ((s8[8388608]{0:T(1024)(128)(4,1)}), s8[4194304]{0:T(1024)(128)(4,1)S(1)}, s32[]{:S(2)}) async-start(s8[8388608]{0:T(1024)(128)(4,1)} %bitcast.47), calls=%async_computation.5 | async-start | bytes 8388608
  134.2 139.1 %copy-start.2 = (f32[2,2048]{1,0:T(2,128)S(1)}, f32[2,2048]{1,0:T(2,128)}, u32[]{:S(2)}) copy-start(f32[2,2048]{1,0:T(2,128)} %param.7) | copy-start | bytes 49156
  134.2 140.4 %slice-start.1 = ((s8[8388608]{0:T(1024)(128)(4,1)}), s8[4194304]{0:T(1024)(128)(4,1)S(1)}, s32[]{:S(2)}) async-start(s8[8388608]{0:T(1024)(128)(4,1)} %bitcast.47), calls=%async_computation.6 | async-start | bytes 8388608
  134.2 46.9 %collective-permute-start.2 = (f32[2,128,2048]{2,1,0:T(8,128)S(1)}, f32[2,128,2048]{2,1,0:T(8,128)S(1)}, u32[]{:S(2)}, u32[]{:S(2)}) collective-permute-start(f32[2,128,2048]{2,1,0:T(8,128)S(1)} %add.55), channel_id=1, source_target_pairs={{0,4},{1,5},{2,6},{3,7},{4,0},{5,1},{6,2},{7,3},{8,12},{9,13},{10,... | collective-permute-start | bytes 6291464 | tf_op jit(solution)/shard_map/ppermute | solution.py:12
  181.4 91.9 %collective-permute-start.3 = (f32[2,128,2048]{2,1,0:T(8,128)S(1)}, f32[2,128,2048]{2,1,0:T(8,128)S(1)}, u32[]{:S(2)}, u32[]{:S(2)}) collective-permute-start(f32[2,128,2048]{2,1,0:T(8,128)S(1)} %add.56), channel_id=1, source_target_pairs={{0,8},{1,9},{2,10},{3,11},{4,12},{5,13},{6,14},{7,15},{8,0},{9,1},... | collective-permute-start | bytes 6291464 | tf_op jit(solution)/shard_map/ppermute | solution.py:12
  275.3 13.4 %copy-start.1 = (bf16[64,1024]{1,0:T(8,128)(2,1)S(1)}, bf16[64,1024]{1,0:T(8,128)(2,1)}, u32[]{:S(2)}) copy-start(bf16[64,1024]{1,0:T(8,128)(2,1)} %reduce-scatter.3.cloned.1.call-done) | copy-start | bytes 393220
Sparse Core Ops, SparseCore 0:
  10.2 40.5 all-gather.1
  57.7 10.7 reduce-scatter.2
  276.9 11.7 reduce-scatter.4
